TPU v7x, 512 devices: a whole 4x8x8 slice. The times are simulated.
512 devices in a mesh: section: 4 (over x), expert: 128 (over y, z, core).
Axes of the slice: x: 4, y: 8, z: 8, core: 2. Of those that a mesh axis runs over, the one named last changes fastest.
Arguments:
- activations: bfloat16 [4, 2, 256, 3072], P('section', None, 'expert'), may hold values from -6 to 6
- routes: int32 [4, 2, 256, 2], P('section', None, 'expert'), may hold values from 0 to 3, all different within a row; in each aligned block of 2 rows (0 to 1, 2 to 3, ..., all dimensions but the last counted through in order) at most 2 rows name the same one
- gate_weights: float32 [4, 2, 256, 2], P('section', None, 'expert'), may hold values from 0.1 to 1
- w_gate: bfloat16 [4, 3072, 32768], P('section', None, 'expert'), may hold values from -0.109375 to 0.109375
- w_up: bfloat16 [4, 3072, 32768], P('section', None, 'expert'), may hold values from -0.109375 to 0.109375
- w_down: bfloat16 [4, 32768, 3072], P('section', 'expert'), may hold values from -0.0625 to 0.0625
Outputs:
- received: bfloat16 [4, 2, 256, 3072], P('section', None, 'expert')
Inputs may be any that keep to these rules, and one draw needn't show every extreme that they name: `routes`: each token names two different experts. Among the 2 tokens of one block of one section and micro-batch, at most 2 name any one expert, and in every draw some block has exactly 2 naming one expert.
All inputs are finite; a program needn't handle non-finite values.
Results may differ from a plain program's by a relative error of at most 0.005.
Values may be sent and summed in bfloat16 or wider, within the bound.
A program may use at most 64 MiB of HBM per device.

v0:
```python
import jax
import jax.numpy as jnp
from jax import lax
from jax.sharding import PartitionSpec as P

EXPERTS = 4
CAP = 2


def shifted(block, axis, distance):
    devices = range(lax.axis_size(axis))
    route = [((i - distance) % len(devices), i) for i in devices]
    return lax.ppermute(block, axis, route)


def on_device(activations, routes, gate_weights, w_gate, w_up, w_down):
    devices = lax.axis_size("expert")
    group_size = devices // EXPERTS
    tokens_all = activations[0]
    routes_all = routes[0]
    weights_all = gate_weights[0]
    gate_cols = w_gate[0]
    up_cols = w_up[0]
    down_rows = w_down[0]
    micros = tokens_all.shape[0]
    model_width = tokens_all.shape[2]
    slot_range = jnp.arange(EXPERTS * CAP, dtype=jnp.int32)
    expert_ids = jnp.arange(EXPERTS, dtype=jnp.int32)

    def slots_of(route_rows):
        onehot = (route_rows[:, :, None] == expert_ids[None, None, :]).astype(jnp.int32)
        member = jnp.sum(onehot, axis=1)
        before = jnp.cumsum(member, axis=0) - member
        position = jnp.sum(onehot * before[:, None, :], axis=2)
        return route_rows * CAP + position

    span_list = [(micro_index, micro_index + 1) for micro_index in range(micros)]
    results = []
    for span_start, span_end in span_list:
        group_width = span_end - span_start
        tok_group = tokens_all[span_start:span_end]
        route_group = routes_all[span_start:span_end]
        weight_group = weights_all[span_start:span_end]
        micro_index = 0
        slot_index = slots_of(route_group[micro_index])
        placement = jnp.sum(
            (slot_range[:, None, None] == slot_index[None, :, :]).astype(jnp.int32), axis=2
        ).astype(jnp.bfloat16)
        buffer = jnp.dot(
            placement, tok_group[micro_index], preferred_element_type=jnp.float32
        ).astype(jnp.bfloat16)
        spread = jnp.broadcast_to(
            buffer.reshape(EXPERTS, 1, CAP, model_width), (EXPERTS, group_size, CAP, model_width)
        )
        send_list = spread.reshape(devices, CAP, model_width)
        row_block = lax.all_to_all(send_list, "expert", split_axis=0, concat_axis=0, tiled=True)
        sources = row_block.shape[0]
        slots_here = row_block.shape[1]
        flat_rows = row_block.reshape(sources * slots_here, model_width)
        gate_proj = jnp.dot(flat_rows, gate_cols, preferred_element_type=jnp.float32)
        up_proj = jnp.dot(flat_rows, up_cols, preferred_element_type=jnp.float32)
        hidden = (jax.nn.silu(gate_proj) * up_proj).astype(jnp.bfloat16)
        partial_value = jnp.dot(hidden, down_rows, preferred_element_type=jnp.float32).astype(
            jnp.bfloat16
        )
        partial_value = partial_value.reshape(sources, slots_here, model_width)
        returned = lax.all_to_all(partial_value, "expert", split_axis=0, concat_axis=0, tiled=True)
        summed = jnp.sum(
            returned.reshape(EXPERTS, group_size, group_width, CAP, model_width).astype(
                jnp.float32
            ),
            axis=1,
        )
        micro_index = 0
        slot_index = slots_of(route_group[micro_index])
        weights = weight_group[micro_index]
        mix_matrix = weights[:, 0, None] * (slot_index[:, 0, None] == slot_range[None, :]).astype(
            jnp.float32
        )
        mix_matrix = mix_matrix + weights[:, 1, None] * (
            slot_index[:, 1, None] == slot_range[None, :]
        ).astype(jnp.float32)
        expert_sum = summed[:, micro_index].reshape(EXPERTS * CAP, model_width)
        combined = jnp.dot(
            mix_matrix,
            expert_sum,
            precision=lax.Precision.HIGHEST,
            preferred_element_type=jnp.float32,
        )
        mixed_rows = (tok_group[micro_index].astype(jnp.float32) + combined).astype(jnp.bfloat16)
        results.append(mixed_rows)
    stacked = jnp.stack(results)[None]
    return shifted(stacked, "section", 1)


def solution(mesh):
    placed = (
        P("section", None, "expert", None),
        P("section", None, "expert", None),
        P("section", None, "expert", None),
        P("section", None, "expert"),
        P("section", None, "expert"),
        P("section", "expert", None),
    )
    return jax.shard_map(
        on_device,
        mesh=mesh,
        in_specs=placed,
        out_specs=P("section", None, "expert", None),
        check_vma=False,
    )
```

profile of v0, /device:TPU:8, one launch (start us, length us, event | category | flops | bytes accessed | tf_op | source)
XLA Modules:
  0.0 222.3 jit_solution(4367435056111999302)
XLA Ops:
  0.0 0.0 copy-start
  0.0 0.8 slice_bitcast_fusion.3
  0.8 0.1 convert_reduce_fusion.3
  1.0 0.1 convert_reduce_fusion.2
  1.1 0.2 select_reduce_fusion
  1.3 0.7 multiply_add_fusion.1
  2.0 0.1 fusion.46
  2.1 0.9 convolution_convert_fusion.3
  3.0 2.0 broadcast_in_dim.11
  5.0 0.0 copy-start.2
  5.0 17.5 %all-to-all-start = ((bf16[128,2,3072]{2,1,0:T(2,128)(2,1)}), bf16[128,2,3072]{2,1,0:T(2,128)(2,1)S(1)}, u32[]{:S(2)}, u32[]{:S(2)}) async-start(bf16[128,2,3072]{2,1,0:T(2,128)(2,1)} %bitcast.68), calls=%async_computation | async-start | bytes 3145728 | tf_op jit(solution)/shard_map/all_to_all | solution.py:56
  22.5 0.1 fusion.47
  22.6 0.0 copy-done.2
  22.6 0.2 convolution_convert_fusion.2
  22.8 41.5 %all-to-all-done = bf16[128,2,3072]{2,1,0:T(2,128)(2,1)S(1)} async-done(((bf16[128,2,3072]{2,1,0:T(2,128)(2,1)}), bf16[128,2,3072]{2,1,0:T(2,128)(2,1)S(1)}, u32[]{:S(2)}, u32[]{:S(2)}) %all-to-all-start) | async-done | bytes 1572896 | tf_op jit(solution)/shard_map/all_to_all | solution.py:56
  64.3 0.0 copy-start.1
  64.3 1.9 broadcast_in_dim.13
  66.3 0.0 copy-done.1
  66.3 7.3 %all-to-all-start.2 = ((bf16[128,2,3072]{2,1,0:T(2,128)(2,1)}), bf16[128,2,3072]{2,1,0:T(2,128)(2,1)}, u32[]{:S(2)}, u32[]{:S(2)}) async-start(bf16[128,2,3072]{2,1,0:T(2,128)(2,1)} %bitcast.67), calls=%async_computation.2 | async-start | bytes 3145728 | tf_op jit(solution)/shard_map/all_to_all | solution.py:56
  73.6 3.7 %reshape.109 = bf16[256,3072]{1,0:T(8,128)(2,1)S(1)} reshape(bf16[128,2,3072]{2,1,0:T(2,128)(2,1)} %copy-done.1) | data formatting | bytes 3145728 | tf_op jit(solution)/shard_map/reshape | solution.py:59
  77.3 2.0 fusion.12
  79.3 0.0 copy-done
  79.3 4.4 %convolution_convert_fusion.1 = bf16[256,3072]{1,0:T(8,128)(2,1)} fusion(bf16[1,256,3072]{2,1,0:T(8,128)(2,1)S(1)} %copy-done, bf16[256,3072]{1,0:T(8,128)(2,1)S(1)} %reshape.109, bf16[1,3072,256]{2,1,0:T(8,128)(2,1)} %param.10, f32[256,256]{1,0:T(8,128)S(1)} %fusion.12), kind=kOutput, calls=%fused_computation.1 | convolution fusion | flops 806486016 | bytes 6553600 | tf_op jit(solution)/shard_map/dot_general | solution.py:63
  83.7 4.5 %reshape.110 = bf16[128,2,3072]{2,1,0:T(2,128)(2,1)} reshape(bf16[256,3072]{1,0:T(8,128)(2,1)} %convolution_convert_fusion.1) | data formatting | bytes 3145728 | tf_op jit(solution)/shard_map/reshape | solution.py:66
  88.2 27.0 %all-to-all-done.2 = bf16[128,2,3072]{2,1,0:T(2,128)(2,1)} async-done(((bf16[128,2,3072]{2,1,0:T(2,128)(2,1)}), bf16[128,2,3072]{2,1,0:T(2,128)(2,1)}, u32[]{:S(2)}, u32[]{:S(2)}) %all-to-all-start.2) | async-done | bytes 1572896 | tf_op jit(solution)/shard_map/all_to_all | solution.py:56
  115.1 7.3 %all-to-all-start.1 = ((bf16[128,2,3072]{2,1,0:T(2,128)(2,1)}), bf16[128,2,3072]{2,1,0:T(2,128)(2,1)}, u32[]{:S(2)}, u32[]{:S(2)}) async-start(bf16[128,2,3072]{2,1,0:T(2,128)(2,1)} %reshape.110), calls=%async_computation.1 | async-start | bytes 3145728 | tf_op jit(solution)/shard_map/all_to_all | solution.py:67
  122.5 3.7 %reshape.112 = bf16[256,3072]{1,0:T(8,128)(2,1)S(1)} reshape(bf16[128,2,3072]{2,1,0:T(2,128)(2,1)} %all-to-all-done.2) | data formatting | bytes 3145728 | tf_op jit(solution)/shard_map/reshape | solution.py:59
  126.1 2.0 fusion.10
  128.1 4.4 %convolution_convert_fusion = bf16[256,3072]{1,0:T(8,128)(2,1)} fusion(bf16[1,256,3072]{2,1,0:T(8,128)(2,1)S(1)} %copy-done, bf16[256,3072]{1,0:T(8,128)(2,1)S(1)} %reshape.112, bf16[1,3072,256]{2,1,0:T(8,128)(2,1)} %param.10, f32[256,256]{1,0:T(8,128)S(1)} %fusion.10), kind=kOutput, calls=%fused_computation | convolution fusion | flops 806486016 | bytes 6553600 | tf_op jit(solution)/shard_map/dot_general | solution.py:63
  132.5 4.5 %reshape.113 = bf16[128,2,3072]{2,1,0:T(2,128)(2,1)} reshape(bf16[256,3072]{1,0:T(8,128)(2,1)} %convolution_convert_fusion) | data formatting | bytes 3145728 | tf_op jit(solution)/shard_map/reshape | solution.py:66
  137.0 0.0 copy-start.3
  137.0 27.0 %all-to-all-done.1 = bf16[128,2,3072]{2,1,0:T(2,128)(2,1)} async-done(((bf16[128,2,3072]{2,1,0:T(2,128)(2,1)}), bf16[128,2,3072]{2,1,0:T(2,128)(2,1)}, u32[]{:S(2)}, u32[]{:S(2)}) %all-to-all-start.1) | async-done | bytes 1572896 | tf_op jit(solution)/shard_map/all_to_all | solution.py:67
  164.0 6.9 %all-to-all-start.3 = ((bf16[128,2,3072]{2,1,0:T(2,128)(2,1)}), bf16[128,2,3072]{2,1,0:T(2,128)(2,1)S(1)}, u32[]{:S(2)}, u32[]{:S(2)}) async-start(bf16[128,2,3072]{2,1,0:T(2,128)(2,1)} %reshape.113), calls=%async_computation.3 | async-start | bytes 3145728 | tf_op jit(solution)/shard_map/all_to_all | solution.py:67
  170.9 0.2 slice_reduce_fusion.7
  171.1 0.2 slice_reduce_fusion.3
  171.3 0.0 copy-done.3
  171.3 0.2 slice_reduce_fusion.6
  171.5 0.2 slice_reduce_fusion.2
  171.7 2.7 %convert_reduce_fusion.1 = f32[4,2,3072]{2,1,0:T(2,128)S(1)} fusion(bf16[128,2,3072]{2,1,0:T(2,128)(2,1)} %all-to-all-done.1), kind=kLoop, calls=%fused_computation.11 | loop fusion | flops 1548288 | bytes 1671168 | tf_op jit(solution)/shard_map/reduce_sum | solution.py:68
  174.4 0.1 reshape_squeeze.6
  174.4 38.3 %all-to-all-done.3 = bf16[128,2,3072]{2,1,0:T(2,128)(2,1)S(1)} async-done(((bf16[128,2,3072]{2,1,0:T(2,128)(2,1)}), bf16[128,2,3072]{2,1,0:T(2,128)(2,1)S(1)}, u32[]{:S(2)}, u32[]{:S(2)}) %all-to-all-start.3) | async-done | bytes 1572896 | tf_op jit(solution)/shard_map/all_to_all | solution.py:67
  212.8 1.3 convert_reduce_fusion
  214.0 0.1 reshape_squeeze.7
  214.1 0.3 fusion.3
  214.4 0.3 fusion.2
  214.8 3.4 %collective-permute-start = (bf16[1,2,2,3072]{3,2,1,0:T(2,128)(2,1)S(1)}, bf16[1,2,2,3072]{3,2,1,0:T(2,128)(2,1)S(1)}, u32[]{:S(2)}, u32[]{:S(2)}) collective-permute-start(bf16[1,2,2,3072]{3,2,1,0:T(2,128)(2,1)S(1)} %maximum_bitcast_fusion), channel_id=1, source_target_pairs={{384,0},{0,128},{128,256},{256,384},{385,1},{1,129},{129,257},{257... | collective-permute-start | bytes 73736 | tf_op jit(solution)/shard_map/ppermute | solution.py:13
  218.2 3.5 %collective-permute-done = bf16[1,2,2,3072]{3,2,1,0:T(2,128)(2,1)S(1)} collective-permute-done((bf16[1,2,2,3072]{3,2,1,0:T(2,128)(2,1)S(1)}, bf16[1,2,2,3072]{3,2,1,0:T(2,128)(2,1)S(1)}, u32[]{:S(2)}, u32[]{:S(2)}) %collective-permute-start) | collective-permute-done | bytes 24608 | tf_op jit(solution)/shard_map/ppermute | solution.py:13
  221.7 0.6 copy.8
  (8 shorter events, 0.2 us)
Async XLA Ops:
  0.0 79.3 %copy-start = (bf16[1,256,3072]{2,1,0:T(8,128)(2,1)S(1)}, bf16[1,256,3072]{2,1,0:T(8,128)(2,1)}, u32[]{:S(2)}) copy-start(bf16[1,256,3072]{2,1,0:T(8,128)(2,1)} %param.11) | copy-start | bytes 4718596
  5.0 17.6 %copy-start.2 = (bf16[1,2,2,3072]{3,2,1,0:T(2,128)(2,1)S(1)}, bf16[1,2,2,3072]{3,2,1,0:T(2,128)(2,1)}, u32[]{:S(2)}) copy-start(bf16[1,2,2,3072]{3,2,1,0:T(2,128)(2,1)} %param.6) | copy-start | bytes 73732
  5.0 59.3 %all-to-all-start = ((bf16[128,2,3072]{2,1,0:T(2,128)(2,1)}), bf16[128,2,3072]{2,1,0:T(2,128)(2,1)S(1)}, u32[]{:S(2)}, u32[]{:S(2)}) async-start(bf16[128,2,3072]{2,1,0:T(2,128)(2,1)} %bitcast.68), calls=%async_computation | async-start | bytes 3145728 | tf_op jit(solution)/shard_map/all_to_all | solution.py:56
  64.3 2.0 copy-start.1
  66.3 48.8 %all-to-all-start.2 = ((bf16[128,2,3072]{2,1,0:T(2,128)(2,1)}), bf16[128,2,3072]{2,1,0:T(2,128)(2,1)}, u32[]{:S(2)}, u32[]{:S(2)}) async-start(bf16[128,2,3072]{2,1,0:T(2,128)(2,1)} %bitcast.67), calls=%async_computation.2 | async-start | bytes 3145728 | tf_op jit(solution)/shard_map/all_to_all | solution.py:56
  115.1 48.9 %all-to-all-start.1 = ((bf16[128,2,3072]{2,1,0:T(2,128)(2,1)}), bf16[128,2,3072]{2,1,0:T(2,128)(2,1)}, u32[]{:S(2)}, u32[]{:S(2)}) async-start(bf16[128,2,3072]{2,1,0:T(2,128)(2,1)} %reshape.110), calls=%async_computation.1 | async-start | bytes 3145728 | tf_op jit(solution)/shard_map/all_to_all | solution.py:67
  137.0 34.3 %copy-start.3 = (f32[1,2,2,2]{3,2,1,0:T(2,128)S(1)}, f32[1,2,2,2]{3,2,1,0:T(2,128)}, u32[]{:S(2)}) copy-start(f32[1,2,2,2]{3,2,1,0:T(2,128)} %param.8) | copy-start | bytes 100
  164.0 48.7 %all-to-all-start.3 = ((bf16[128,2,3072]{2,1,0:T(2,128)(2,1)}), bf16[128,2,3072]{2,1,0:T(2,128)(2,1)S(1)}, u32[]{:S(2)}, u32[]{:S(2)}) async-start(bf16[128,2,3072]{2,1,0:T(2,128)(2,1)} %reshape.113), calls=%async_computation.3 | async-start | bytes 3145728 | tf_op jit(solution)/shard_map/all_to_all | solution.py:67
  214.8 6.9 %collective-permute-start = (bf16[1,2,2,3072]{3,2,1,0:T(2,128)(2,1)S(1)}, bf16[1,2,2,3072]{3,2,1,0:T(2,128)(2,1)S(1)}, u32[]{:S(2)}, u32[]{:S(2)}) collective-permute-start(bf16[1,2,2,3072]{3,2,1,0:T(2,128)(2,1)S(1)} %maximum_bitcast_fusion), channel_id=1, source_target_pairs={{384,0},{0,128},{128,256},{256,384},{385,1},{1,129},{129,257},{257... | collective-permute-start | bytes 73736 | tf_op jit(solution)/shard_map/ppermute | solution.py:13
where the time goes:
time: 223 us; the launch traced here: 222 us
  waiting for transfers between devices  137 us (61%)
  starting transfers between devices  42.4 us (19%)
  local copies, waits for them, and re-layouts  22.5 us (10%)
  matrix products  14.5 us (7%)
  other arithmetic  5.37 us (2%)
    all_to_all x2, waiting for transfers between devices, on_device(): lax.all_to_all(send_list, 'expert', split_axis=0, concat_axis=0, tiled=True)  68.5 us
    all_to_all x2, waiting for transfers between devices, on_device(): lax.all_to_all(partial_value, 'expert', split_axis=0, concat_axis=0, tile...  65.3 us
    all_to_all x2, starting transfers between devices, on_device(): lax.all_to_all(send_list, 'expert', split_axis=0, concat_axis=0, tiled=True)  24.8 us
    all_to_all x2, starting transfers between devices, on_device(): lax.all_to_all(partial_value, 'expert', split_axis=0, concat_axis=0, tile...  14.2 us
    reshape x2, local copies, waits for them, and re-layouts, on_device(): partial_value = partial_value.reshape(sources, slots_here, model_width)  8.98 us
    dot_general x2, matrix products, on_device(): jnp.dot(hidden, down_rows, preferred_element_type=jnp.float32)  8.83 us
    reshape x2, local copies, waits for them, and re-layouts, on_device(): flat_rows = row_block.reshape(sources * slots_here, model_width)  7.3 us
  transfers between devices with their start and end apart: 5, of which 5 were waited for; matrix products, arithmetic and copies ran while one was open for 15% of the time, Pallas kernels for 0%

commit v1 on v0

v1 whole, which is shorter than its diff:
```python
import jax
import jax.numpy as jnp
from jax import lax
from jax.experimental import pallas as pl
from jax.experimental.pallas import tpu as pltpu
from jax.sharding import PartitionSpec as P

EXPERTS = 4
MICRO = 2
ROWS = 2
D = 3072
HID = 256
RING = 8
LANES = 128
TILES = D // LANES
WIDE = TILES + 1
UNIT = RING * ROWS
SLOT = {0: 0, 1: 1, -1: 2, 2: 3, -2: 4, 3: 5, -3: 6, 4: 7, -4: 7}
MESH = pl.DeviceIdType.MESH
F32 = jnp.float32
BF16 = jnp.bfloat16


def layer_kernel(own_ref, gate_hbm, up_hbm, down_hbm, out_ref,
                 xb, xr, gate_w, up_w, down_w, hid, part, recv, summed, back, final,
                 w_sem, ws_sem, wr_sem, fs_sem, fr_sem, as_sem, ar_sem,
                 rs_sem, rr_sem, bs_sem, br_sem, xs_sem, xr_sem, own_sem):
    section = lax.axis_index("section")
    place = lax.axis_index("expert")
    core = lax.rem(place, 2)
    z = lax.rem(place // 2, RING)
    y = place // (2 * RING)
    first = core == 0
    f_pos = z * (1 - core) + y * core
    g_pos = y * (1 - core) + z * core
    f_step = 1 + (RING - 1) * core
    g_step = RING - (RING - 1) * core
    expert = y // 2

    def at(f, g):
        return (section, (f * f_step + g * g_step) * 2 + core)

    def f_peer(k):
        return at(lax.rem(f_pos + k, RING), g_pos)

    sibling = (section, place + 1 - 2 * core)
    g_next = at(f_pos, lax.rem(g_pos + 1, RING))
    g_prev = at(f_pos, lax.rem(g_pos + RING - 1, RING))
    x_next = (lax.rem(section + 1, 4), place)
    x_prev = (lax.rem(section + 3, 4), place)

    hbm = (gate_hbm, up_hbm, down_hbm)
    held = (gate_w, up_w, down_w)
    own_copies = [pltpu.make_async_copy(hbm[i], held[i].at[0], w_sem.at[i]) for i in range(3)]
    for copy in own_copies:
        copy.start()
    own_block = [pltpu.make_async_copy(own_ref.at[m], xb.at[0, m, :, f_pos], own_sem.at[m]) for m in range(MICRO)]
    for copy in own_block:
        copy.start()

    barrier = pltpu.get_barrier_semaphore()
    partners = [f_peer(k) for k in range(1, RING)] + [g_next, g_prev, sibling, x_next, x_prev]
    for partner in partners:
        pl.semaphore_signal(barrier, inc=1, device_id=partner, device_id_type=MESH)
    pl.semaphore_wait(barrier, len(partners))

    f_out = []
    for m in range(MICRO):
        for k in (4, 3, 5, 2, 6, 1, 7):
            copy = pltpu.make_async_remote_copy(
                src_ref=own_ref.at[m], dst_ref=xb.at[0, m, :, f_pos],
                send_sem=fs_sem.at[m, k], recv_sem=fr_sem.at[m, k],
                device_id=f_peer(k), device_id_type=MESH)
            copy.start()
            f_out.append(copy)
    w_out = []
    for i in range(3):
        copy = pltpu.make_async_remote_copy(
            src_ref=hbm[i], dst_ref=held[i].at[1], send_sem=ws_sem.at[i], recv_sem=wr_sem.at[i],
            device_id=sibling, device_id_type=MESH)
        copy.start()
        w_out.append(copy)

    def g_copy(way, step, m):
        src = SLOT[-step * way]
        dst = SLOT[-(step + 1) * way]
        j = 0 if way == 1 else 1
        return pltpu.make_async_remote_copy(
            src_ref=xb.at[src, m], dst_ref=xb.at[dst, m],
            send_sem=as_sem.at[j, step, m], recv_sem=ar_sem.at[j, step, m],
            device_id=g_next if way == 1 else g_prev, device_id_type=MESH)

    def widen(slot, m):
        view = xb.at[slot, m].reshape(WIDE, UNIT, LANES)
        row = (slot * MICRO + m) * UNIT
        for t in range(WIDE):
            xr[row:row + UNIT, t * LANES:(t + 1) * LANES] = view[t]

    pick = lax.broadcasted_iota(jnp.int32, (LANES, HID), 0)
    pick = jnp.where((pick == expert) | (pick == expert + EXPERTS), 1.0, 0.0).astype(BF16)

    def compute(low, high):
        rows = slice(low * MICRO * UNIT, high * MICRO * UNIT)
        weight = jnp.dot(xr[rows, D:], pick, preferred_element_type=F32)
        for side in range(2):
            gate = jnp.dot(xr[rows, :D], gate_w[side], preferred_element_type=F32)
            up = jnp.dot(xr[rows, :D], up_w[side], preferred_element_type=F32)
            value = gate / (1.0 + jnp.exp(-gate)) * up * weight
            hid[rows, side * HID:(side + 1) * HID] = value.astype(BF16)
        for t in range(D // 256):
            cols = slice(t * 256, (t + 1) * 256)
            total = jnp.dot(hid[rows, :HID], down_w[0, :, cols], preferred_element_type=F32)
            total = total + jnp.dot(hid[rows, HID:], down_w[1, :, cols], preferred_element_type=F32)
            part[rows, cols] = total.astype(BF16)

    g_out = []
    for m in range(MICRO):
        own_block[m].wait()
        for k in range(1, RING):
            pltpu.make_async_remote_copy(
                src_ref=own_ref.at[m], dst_ref=xb.at[0, m, :, f_pos],
                send_sem=fs_sem.at[m, k], recv_sem=fr_sem.at[m, k],
                device_id=f_peer(k), device_id_type=MESH).wait_recv()
        for way in (1, -1):
            copy = g_copy(way, 0, m)
            copy.start()
            g_out.append(copy)
    for m in range(MICRO):
        widen(0, m)
    for step in range(1, 4):
        for m in range(MICRO):
            for way in (1, -1):
                g_copy(way, step - 1, m).wait_recv()
                if step < 3 or m == (0 if way == 1 else 1):
                    copy = g_copy(way, step, m)
                    copy.start()
                    g_out.append(copy)
        for m in range(MICRO):
            for way in (1, -1):
                widen(SLOT[-step * way], m)
        if step == 2:
            for i in range(3):
                own_copies[i].wait()
                w_out[i].wait()
            compute(0, 3)
        if step == 3:
            compute(3, 5)
    g_copy(1, 3, 0).wait_recv()
    g_copy(-1, 3, 1).wait_recv()
    for m in range(MICRO):
        widen(SLOT[4], m)
    compute(5, 8)

    def unit(slot, m):
        row = (slot * MICRO + m) * UNIT
        return part.at[row:row + UNIT]

    def back_copy(way, dist, m):
        j = 0 if way == 1 else 1
        return pltpu.make_async_remote_copy(
            src_ref=unit(SLOT[dist * way], m), dst_ref=recv.at[j, dist - 1, m],
            send_sem=rs_sem.at[j, dist - 1, m], recv_sem=rr_sem.at[j, dist - 1, m],
            device_id=g_next if way == 1 else g_prev, device_id_type=MESH)

    for dist in range(4, 0, -1):
        for m in range(MICRO):
            for way in (1, -1):
                j = 0 if way == 1 else 1
                if dist == 4 and m != j:
                    continue
                if dist < 3 or (dist == 3 and m == j):
                    back_copy(way, dist + 1, m).wait_recv()
                    here = unit(SLOT[dist * way], m)
                    here[...] = (here[...].astype(F32) + recv[j, dist, m].astype(F32)).astype(BF16)
                copy = back_copy(way, dist, m)
                copy.start()
                g_out.append(copy)
    for m in range(MICRO):
        back_copy(1, 1, m).wait_recv()
        back_copy(-1, 1, m).wait_recv()
        here = unit(0, m)
        for t in range(TILES):
            cols = slice(t * LANES, (t + 1) * LANES)
            total = here[:, cols].astype(F32) + recv[0, 0, m, :, cols].astype(F32) + recv[1, 0, m, :, cols].astype(F32)
            summed.at[m].reshape(TILES, UNIT, LANES)[t] = total.astype(BF16)

    def f_back(k):
        return pltpu.make_async_remote_copy(
            src_ref=summed.at[:, :, lax.rem(f_pos + k, RING)], dst_ref=back.at[k],
            send_sem=bs_sem.at[k], recv_sem=br_sem.at[k],
            device_id=f_peer(k), device_id_type=MESH)

    for k in (4, 3, 5, 2, 6, 1, 7):
        copy = f_back(k)
        copy.start()
        g_out.append(copy)
    keep = pltpu.make_async_copy(summed.at[:, :, f_pos], back.at[0], br_sem.at[0])
    keep.start()
    keep.wait()
    total = own_ref[:, :TILES].astype(F32) + back[0].astype(F32)
    for k in (1, 7, 2, 6, 3, 5, 4):
        f_back(k).wait_recv()
        total = total + back[k].astype(F32)
    final[...] = total.astype(BF16)
    last = pltpu.make_async_remote_copy(
        src_ref=final, dst_ref=out_ref, send_sem=xs_sem, recv_sem=xr_sem,
        device_id=x_next, device_id_type=MESH)
    last.start()
    for copy in f_out + g_out:
        copy.wait_send()
    last.wait()


def on_device(activations, routes, gate_weights, w_gate, w_up, w_down):
    tokens = activations[0].reshape(MICRO, ROWS, TILES, LANES).transpose(0, 2, 1, 3)
    named = (routes[0][..., None] == jnp.arange(EXPERTS, dtype=jnp.int32)).astype(F32)
    weight = jnp.sum(gate_weights[0][..., None] * named, axis=2)
    high = lax.reduce_precision(weight, 8, 7)
    low = weight - high
    extra = jnp.concatenate([high, low], axis=-1).astype(BF16)
    extra = jnp.pad(extra, ((0, 0), (0, 0), (0, LANES - 2 * EXPERTS)))
    own = jnp.concatenate([tokens, extra[:, None]], axis=1)
    dma = pltpu.SemaphoreType.DMA
    vmem = pltpu.VMEM
    out = pl.pallas_call(
        layer_kernel,
        out_shape=jax.ShapeDtypeStruct((MICRO, TILES, ROWS, LANES), BF16),
        in_specs=[pl.BlockSpec(memory_space=pltpu.VMEM)] + [pl.BlockSpec(memory_space=pl.ANY)] * 3,
        out_specs=pl.BlockSpec(memory_space=pltpu.VMEM),
        scratch_shapes=[
            vmem((RING, MICRO, WIDE, RING, ROWS, LANES), BF16),
            vmem((RING * MICRO * UNIT, WIDE * LANES), BF16),
            vmem((2, D, HID), BF16),
            vmem((2, D, HID), BF16),
            vmem((2, HID, D), BF16),
            vmem((RING * MICRO * UNIT, 2 * HID), BF16),
            vmem((RING * MICRO * UNIT, D), BF16),
            vmem((2, 4, MICRO, UNIT, D), BF16),
            vmem((MICRO, TILES, RING, ROWS, LANES), BF16),
            vmem((RING, MICRO, TILES, ROWS, LANES), BF16),
            vmem((MICRO, TILES, ROWS, LANES), BF16),
            dma((3,)), dma((3,)), dma((3,)),
            dma((MICRO, RING)), dma((MICRO, RING)),
            dma((2, 4, MICRO)), dma((2, 4, MICRO)),
            dma((2, 4, MICRO)), dma((2, 4, MICRO)),
            dma((RING,)), dma((RING,)),
            dma, dma, dma((MICRO,)),
        ],
        compiler_params=pltpu.CompilerParams(
            collective_id=0, has_side_effects=True, vmem_limit_bytes=56 << 20),
    )(own, w_gate[0], w_up[0], w_down[0])
    return out.transpose(0, 2, 1, 3).reshape(1, MICRO, ROWS, D)


def solution(mesh):
    placed = (
        P("section", None, "expert", None),
        P("section", None, "expert", None),
        P("section", None, "expert", None),
        P("section", None, "expert"),
        P("section", None, "expert"),
        P("section", "expert", None),
    )
    return jax.shard_map(
        on_device,
        mesh=mesh,
        in_specs=placed,
        out_specs=P("section", None, "expert", None),
        check_vma=False,
    )
```

time: 223 us -> 72.1 us (0.32)
  waiting for transfers between devices: 137 us -> 0 us
  Pallas kernels: 0 us -> 68.1 us
  starting transfers between devices: 42.4 us -> 0 us
  local copies, waits for them, and re-layouts: 22.5 us -> 1.36 us
  matrix products: 14.5 us -> 0 us
  other arithmetic: 5.37 us -> 2.24 us
    all_to_all x4 -> x0, waiting for transfers between devices: 134 us -> none  [the longest x2 68.5 us: on_device(): lax.all_to_all(send_list, 'expert', split_axis=0, concat_axis=0, tiled=True)]
    pallas_call x0 -> x1, Pallas kernels: none -> 68.1 us  [on_device(): pl.pallas_call(layer_kernel, out_shape=jax.ShapeDtypeStruct((MICRO, TILES...]
    all_to_all x4 -> x0, starting transfers between devices: 39 us -> none  [the longest x2 24.8 us: on_device(): lax.all_to_all(send_list, 'expert', split_axis=0, concat_axis=0, tiled=True)]
    reshape x4 -> x0, local copies, waits for them, and re-layouts: 16.3 us -> none  [the longest x2 8.98 us: on_device(): partial_value = partial_value.reshape(sources, slots_here, model_width)]
    dot_general x8 -> x0, matrix products: 14.5 us -> none  [the longest x2 8.83 us: on_device(): jnp.dot(hidden, down_rows, preferred_element_type=jnp.float32)]
    broadcast_in_dim x4 -> x0, local copies, waits for them, and re-layouts: 3.96 us -> none  [on_device(): jnp.broadcast_to(buffer.reshape(EXPERTS, 1, CAP, model_width), (EXPERTS,...]
    reduce_sum x7 -> x1, other arithmetic: 4.54 us -> 0.78 us  [on_device(): weight = jnp.sum(gate_weights[0][..., None] * named, axis=2)]
    ppermute x1 -> x0, waiting for transfers between devices: 3.52 us -> none  [shifted(): return lax.ppermute(block, axis, route)]
  transfers between devices with their start and end apart: 5 -> 0, of which waited for: 5 -> 0; matrix products, arithmetic and copies ran while one was open for 15% -> 0% of each run, Pallas kernels for 0% -> 0%
where the time goes in v1:
time: 72.1 us; the launch traced here: 71.8 us
  Pallas kernels  68.1 us (94%)
  other arithmetic  2.24 us (3%)
  local copies, waits for them, and re-layouts  1.36 us (2%)
    pallas_call x1, Pallas kernels, on_device(): pl.pallas_call(layer_kernel, out_shape=jax.ShapeDtypeStruct((MICRO, TILES...  68.1 us

profile of v1, /device:TPU:8, one launch (start us, length us, event | category | flops | bytes accessed | tf_op | source)
XLA Modules:
  0.0 71.8 jit_solution(8951923333022207432)
XLA Ops:
  0.0 0.8 %fusion = f32[2,2,4]{2,1,0:T(2,128)S(1)} fusion(f32[2,2,2]{2,1,0:T(2,128)} %bitcast.18, s32[2,2,2]{2,1,0:T(2,128)} %bitcast.19), kind=kLoop, calls=%fused_computation.2 | loop fusion | flops 80 | bytes 128 | tf_op jit(solution)/shard_map/reduce_sum | solution.py:217
  0.8 0.1 fusion.5
  0.9 1.4 %pad_maximum_fusion.own_ref = bf16[2,25,2,128]{3,2,1,0:T(2,128)(2,1)} fusion(bf16[2,1,2,128]{3,2,1,0:T(2,128)(2,1)S(1)} %fusion.5, bf16[2,24,2,128]{3,2,1,0:T(2,128)(2,1)} %bitcast.17), kind=kLoop, calls=%fused_computation | loop fusion | flops 12800 | bytes 51200 | tf_op jit(solution)/shard_map/concatenate | solution.py:222
  2.2 68.1 %shard_map.64 = bf16[2,24,2,128]{3,2,1,0:T(2,128)(2,1)} custom-call(bf16[2,25,2,128]{3,2,1,0:T(2,128)(2,1)} %pad_maximum_fusion.own_ref, bf16[3072,256]{1,0:T(8,128)(2,1)} %bitcast.13, bf16[3072,256]{1,0:T(8,128)(2,1)} %bitcast.14, bf16[256,3072]{1,0:T(8,128)(2,1)} %bitcast.15), custom_call_target="tpu_custom_call" | custom-call | tf_op jit(solution)/shard_map/pallas_call | solution.py:225
  70.4 1.4 %copy.8 = bf16[1,2,2,3072]{3,2,1,0:T(2,128)(2,1)} copy(bf16[1,2,2,3072]{3,2,1,0:T(2,128)(2,1)} %bitcast.16) | data formatting | bytes 49152
  (1 shorter events, 0.0 us)

commit v2 on v1

v2 whole, which is shorter than its diff:
```python
import jax
import jax.numpy as jnp
from jax import lax
from jax.experimental import pallas as pl
from jax.experimental.pallas import tpu as pltpu
from jax.sharding import PartitionSpec as P

EXPERTS = 4
MICRO = 2
ROWS = 2
D = 3072
HID = 256
RING = 8
LANES = 128
TILES = D // LANES
WIDE = TILES + 1
UNIT = RING * ROWS
SLOT = {0: 0, 1: 1, -1: 2, 2: 3, -2: 4, 3: 5, -3: 6, 4: 7, -4: 7}
MESH = pl.DeviceIdType.MESH
F32 = jnp.float32
BF16 = jnp.bfloat16


ORDER = (0, 1, 7, 2, 6, 3, 5, 4)
SEAT = {k: i for i, k in enumerate(ORDER)}
GROUPS = ((0, 1), (1, 3), (3, 5), (5, 8))
WAYS = (1, -1)
HALF = RING * UNIT


def layer_kernel(act_hbm, routes_ref, weights_ref, gate_hbm, up_hbm, down_hbm, out_ref,
                 xb, xr, gate_w, up_w, down_w, hid, part, recv, summed, back, final,
                 w_sem, ws_sem, wr_sem, fs_sem, fr_sem, as_sem, ar_sem,
                 rs_sem, rr_sem, bs_sem, br_sem, xs_sem, xr_sem, own_sem):
    section = lax.axis_index("section")
    place = lax.axis_index("expert")
    core = lax.rem(place, 2)
    z = lax.rem(place // 2, RING)
    y = place // (2 * RING)
    f_pos = z * (1 - core) + y * core
    g_pos = y * (1 - core) + z * core
    f_step = 1 + (RING - 1) * core
    g_step = RING - (RING - 1) * core
    expert = y // 2

    def at(f, g):
        return (section, (f * f_step + g * g_step) * 2 + core)

    def f_peer(k):
        return at(lax.rem(f_pos + k, RING), g_pos)

    def g_peer(k):
        return at(f_pos, lax.rem(g_pos + RING + k, RING))

    sibling = (section, place + 1 - 2 * core)
    x_next = (lax.rem(section + 1, 4), place)
    x_prev = (lax.rem(section + 3, 4), place)

    barrier = pltpu.get_barrier_semaphore()
    partners = [f_peer(k) for k in range(1, RING)] + [g_peer(k) for k in (1, -1, 2, -2)] + [sibling, x_next, x_prev]
    for partner in partners:
        pl.semaphore_signal(barrier, inc=1, device_id=partner, device_id_type=MESH)

    hbm = (gate_hbm, up_hbm, down_hbm)
    held = (gate_w, up_w, down_w)
    own_block = pltpu.make_async_copy(act_hbm, xb.at[0, :, 0:TILES, 0], own_sem)
    own_block.start()
    own_copies = [pltpu.make_async_copy(hbm[i], held[i].at[0], w_sem.at[i]) for i in range(3)]
    for copy in own_copies:
        copy.start()
    lane = lax.broadcasted_iota(jnp.int32, (ROWS, LANES), 1)
    for m in range(MICRO):
        weight = jnp.zeros((ROWS, LANES), F32)
        for k in range(2):
            named = (lax.rem(lane, EXPERTS) == routes_ref[m, :, k:k + 1]) & (lane < 2 * EXPERTS)
            weight = weight + jnp.where(named, weights_ref[m, :, k:k + 1], 0.0)
        high = weight.astype(BF16)
        low = (weight - high.astype(F32)).astype(BF16)
        xb[0, m, TILES, 0] = jnp.where(lane < EXPERTS, high.astype(F32), low.astype(F32)).astype(BF16)
    own_block.wait()
    pl.semaphore_wait(barrier, len(partners))

    def f_copy(m, k):
        return pltpu.make_async_remote_copy(
            src_ref=xb.at[0, m, :, 0], dst_ref=xb.at[0, m, :, SEAT[RING - k]],
            send_sem=fs_sem.at[m, k], recv_sem=fr_sem.at[m, RING - k],
            device_id=f_peer(k), device_id_type=MESH)

    def f_wait(m, k):
        pltpu.make_async_remote_copy(
            src_ref=xb.at[0, m, :, 0], dst_ref=xb.at[0, m, :, SEAT[k]],
            send_sem=fs_sem.at[m, k], recv_sem=fr_sem.at[m, k],
            device_id=f_peer(k), device_id_type=MESH).wait_recv()

    sent = []

    def start(copy):
        copy.start()
        sent.append(copy)

    def g_copy(way, dist, m, group):
        low, high = GROUPS[group]
        j = 0 if way == 1 else 1
        hops = 2 if dist == 4 else 1
        return pltpu.make_async_remote_copy(
            src_ref=xb.at[SLOT[-(dist - hops) * way], m, :, low:high],
            dst_ref=xb.at[SLOT[-dist * way], m, :, low:high],
            send_sem=as_sem.at[j, dist - 1, m, group], recv_sem=ar_sem.at[j, dist - 1, m, group],
            device_id=g_peer(hops * way), device_id_type=MESH)

    def far(way, m):
        return m == (0 if way == 1 else 1)

    def spread(group):
        for m in range(MICRO):
            for way in WAYS:
                start(g_copy(way, 1, m, group))

    def relay(dist, group):
        for m in range(MICRO):
            for way in WAYS:
                g_copy(way, dist, m, group).wait_recv()
                if dist == 2 and far(way, m):
                    start(g_copy(way, 4, m, group))
                start(g_copy(way, dist + 1, m, group))

    def widen(slot, m):
        view = xb.at[slot, m].reshape(WIDE, UNIT, LANES)
        row = m * HALF + slot * UNIT
        for t in range(WIDE):
            xr[row:row + UNIT, t * LANES:(t + 1) * LANES] = view[t]

    pick = lax.broadcasted_iota(jnp.int32, (LANES, HID), 0)
    pick = jnp.where((pick == expert) | (pick == expert + EXPERTS), 1.0, 0.0).astype(BF16)

    def compute(m, low, high):
        rows = slice(m * HALF + low * UNIT, m * HALF + high * UNIT)
        weight = jnp.dot(xr[rows, D:], pick, preferred_element_type=F32)
        for side in range(2):
            gate = jnp.dot(xr[rows, :D], gate_w[side], preferred_element_type=F32)
            up = jnp.dot(xr[rows, :D], up_w[side], preferred_element_type=F32)
            value = gate / (1.0 + jnp.exp(-gate)) * up * weight
            hid[rows, side * HID:(side + 1) * HID] = value.astype(BF16)
        for t in range(D // 256):
            cols = slice(t * 256, (t + 1) * 256)
            total = jnp.dot(hid[rows, :HID], down_w[0, :, cols], preferred_element_type=F32)
            total = total + jnp.dot(hid[rows, HID:], down_w[1, :, cols], preferred_element_type=F32)
            part[rows, cols] = total.astype(BF16)

    for m in range(MICRO):
        for k in (4, 3, 5, 2, 6, 1, 7):
            start(f_copy(m, k))
    spread(0)
    w_out = []
    for i in range(3):
        copy = pltpu.make_async_remote_copy(
            src_ref=hbm[i], dst_ref=held[i].at[1], send_sem=ws_sem.at[i], recv_sem=wr_sem.at[i],
            device_id=sibling, device_id_type=MESH)
        copy.start()
        w_out.append(copy)

    def spread_from(group):
        for m in range(MICRO):
            for i in range(*GROUPS[group]):
                f_wait(m, ORDER[i])
            for way in WAYS:
                start(g_copy(way, 1, m, group))

    spread_from(1)
    relay(1, 0)
    spread_from(2)
    relay(1, 1)
    spread_from(3)
    relay(2, 0)
    relay(1, 2)
    relay(2, 1)
    relay(1, 3)
    relay(2, 2)
    relay(2, 3)
    for i in range(3):
        own_copies[i].wait()
        w_out[i].wait()
    for m in range(MICRO):
        for slot in range(5):
            widen(slot, m)
        compute(m, 0, 5)

    def unit(slot, m):
        row = m * HALF + slot * UNIT
        return part.at[row:row + UNIT]

    def back_copy(way, dist, m):
        j = 0 if way == 1 else 1
        return pltpu.make_async_remote_copy(
            src_ref=unit(SLOT[dist * way], m), dst_ref=recv.at[j, dist - 1, m],
            send_sem=rs_sem.at[j, dist - 1, m], recv_sem=rr_sem.at[j, dist - 1, m],
            device_id=g_peer(2 * way if dist == 4 else way), device_id_type=MESH)

    for m in range(MICRO):
        for way in WAYS:
            for group in range(4):
                g_copy(way, 3, m, group).wait_recv()
                if far(way, m):
                    g_copy(way, 4, m, group).wait_recv()
        for slot in range(5, 8):
            widen(slot, m)
        compute(m, 5, 8)
        for way in WAYS:
            if far(way, m):
                start(back_copy(way, 4, m))
            start(back_copy(way, 3, m))
    for dist in (2, 1):
        for m in range(MICRO):
            for way in WAYS:
                j = 0 if way == 1 else 1
                back_copy(way, dist + 1, m).wait_recv()
                here = unit(SLOT[dist * way], m)
                total = here[...].astype(F32) + recv[j, dist, m].astype(F32)
                if dist == 2 and far(way, m):
                    back_copy(way, 4, m).wait_recv()
                    total = total + recv[j, 3, m].astype(F32)
                here[...] = total.astype(BF16)
                start(back_copy(way, dist, m))

    def f_back(m, k):
        return pltpu.make_async_remote_copy(
            src_ref=summed.at[m, :, SEAT[k]], dst_ref=back.at[m, :, SEAT[RING - k]],
            send_sem=bs_sem.at[m, k], recv_sem=br_sem.at[m, RING - k],
            device_id=f_peer(k), device_id_type=MESH)

    def f_back_wait(m, k):
        pltpu.make_async_remote_copy(
            src_ref=summed.at[m, :, SEAT[k]], dst_ref=back.at[m, :, SEAT[k]],
            send_sem=bs_sem.at[m, k], recv_sem=br_sem.at[m, k],
            device_id=f_peer(k), device_id_type=MESH).wait_recv()

    for m in range(MICRO):
        back_copy(1, 1, m).wait_recv()
        back_copy(-1, 1, m).wait_recv()
        here = unit(0, m)
        for t in range(TILES):
            cols = slice(t * LANES, (t + 1) * LANES)
            total = here[:, cols].astype(F32) + recv[0, 0, m, :, cols].astype(F32) + recv[1, 0, m, :, cols].astype(F32)
            summed.at[m].reshape(TILES, UNIT, LANES)[t] = total.astype(BF16)
        for k in (4, 3, 5, 2, 6, 1, 7):
            start(f_back(m, k))
    last = [pltpu.make_async_remote_copy(
        src_ref=final.at[m], dst_ref=out_ref.at[m], send_sem=xs_sem.at[m], recv_sem=xr_sem.at[m],
        device_id=x_next, device_id_type=MESH) for m in range(MICRO)]
    for m in range(MICRO):
        total = xb[0, m, 0:TILES, 0].astype(F32) + summed[m, :, 0].astype(F32)
        for k in (1, 7, 2, 6, 3, 5, 4):
            f_back_wait(m, k)
            total = total + back[m, :, SEAT[k]].astype(F32)
        final[m] = total.astype(BF16)
        last[m].start()
    for copy in sent:
        copy.wait_send()
    for m in range(MICRO):
        last[m].wait()


def on_device(activations, routes, gate_weights, w_gate, w_up, w_down):
    tokens = activations[0].reshape(MICRO, ROWS, TILES, LANES).transpose(0, 2, 1, 3)
    dma = pltpu.SemaphoreType.DMA
    vmem = pltpu.VMEM
    out = pl.pallas_call(
        layer_kernel,
        out_shape=jax.ShapeDtypeStruct((MICRO, TILES, ROWS, LANES), BF16),
        in_specs=[pl.BlockSpec(memory_space=pl.ANY)] + [pl.BlockSpec(memory_space=pltpu.VMEM)] * 2
        + [pl.BlockSpec(memory_space=pl.ANY)] * 3,
        out_specs=pl.BlockSpec(memory_space=pltpu.VMEM),
        scratch_shapes=[
            vmem((RING, MICRO, WIDE, RING, ROWS, LANES), BF16),
            vmem((MICRO * HALF, WIDE * LANES), BF16),
            vmem((2, D, HID), BF16),
            vmem((2, D, HID), BF16),
            vmem((2, HID, D), BF16),
            vmem((MICRO * HALF, 2 * HID), BF16),
            vmem((MICRO * HALF, D), BF16),
            vmem((2, 4, MICRO, UNIT, D), BF16),
            vmem((MICRO, TILES, RING, ROWS, LANES), BF16),
            vmem((MICRO, TILES, RING, ROWS, LANES), BF16),
            vmem((MICRO, TILES, ROWS, LANES), BF16),
            dma((3,)), dma((3,)), dma((3,)),
            dma((MICRO, RING)), dma((MICRO, RING)),
            dma((2, 4, MICRO, 4)), dma((2, 4, MICRO, 4)),
            dma((2, 4, MICRO)), dma((2, 4, MICRO)),
            dma((MICRO, RING)), dma((MICRO, RING)),
            dma((MICRO,)), dma((MICRO,)), dma,
        ],
        compiler_params=pltpu.CompilerParams(
            collective_id=0, has_side_effects=True, vmem_limit_bytes=56 << 20),
    )(tokens, routes[0], gate_weights[0], w_gate[0], w_up[0], w_down[0])
    return out.transpose(0, 2, 1, 3).reshape(1, MICRO, ROWS, D)


def solution(mesh):
    placed = (
        P("section", None, "expert", None),
        P("section", None, "expert", None),
        P("section", None, "expert", None),
        P("section", None, "expert"),
        P("section", None, "expert"),
        P("section", "expert", None),
    )
    return jax.shard_map(
        on_device,
        mesh=mesh,
        in_specs=placed,
        out_specs=P("section", None, "expert", None),
        check_vma=False,
    )
```

time: 72.1 us -> 65.9 us (0.914)
  Pallas kernels: 68.1 us -> 64.3 us
  other arithmetic: 2.24 us -> 0 us
    pallas_call x1, Pallas kernels: 68.1 us -> 64.3 us  [on_device(): pl.pallas_call(layer_kernel, out_shape=jax.ShapeDtypeStruct((MICRO, TILES...]
    concatenate x1 -> x0, other arithmetic: 1.37 us -> none  [on_device(): own = jnp.concatenate([tokens, extra[:, None]], axis=1)]
    reduce_sum x1 -> x0, other arithmetic: 0.78 us -> none  [on_device(): weight = jnp.sum(gate_weights[0][..., None] * named, axis=2)]
where the time goes in v2:
time: 65.9 us; the launch traced here: 65.7 us
  Pallas kernels  64.3 us (98%)
  local copies, waits for them, and re-layouts  1.36 us (2%)
    pallas_call x1, Pallas kernels, on_device(): pl.pallas_call(layer_kernel, out_shape=jax.ShapeDtypeStruct((MICRO, TILES...  64.3 us
    unnamed x1, local copies, waits for them, and re-layouts  1.36 us

profile of v2, /device:TPU:8, one launch (start us, length us, event | category | flops | bytes accessed | tf_op | source)
XLA Modules:
  0.0 65.7 jit_solution(6343717756933612665)
XLA Ops:
  0.0 64.3 %shard_map.64 = bf16[2,24,2,128]{3,2,1,0:T(2,128)(2,1)} custom-call(bf16[2,24,2,128]{3,2,1,0:T(2,128)(2,1)} %bitcast.15, s32[2,2,2]{2,1,0:T(2,128)} %bitcast.16, f32[2,2,2]{2,1,0:T(2,128)} %bitcast.17, bf16[3072,256]{1,0:T(8,128)(2,1)} %bitcast.11, bf16[3072,256]{1,0:T(8,128)(2,1)} %bitcast.12, bf16[256,3072]{1,0:T(8,128)(2,1)} %bitcast.13), custom_call_target="tpu_custom_call" | custom-call | tf_op jit(solution)/shard_map/pallas_call | solution.py:267
  64.3 1.4 %copy.8 = bf16[1,2,2,3072]{3,2,1,0:T(2,128)(2,1)} copy(bf16[1,2,2,3072]{3,2,1,0:T(2,128)(2,1)} %bitcast.14) | data formatting | bytes 49152

commit v3 on v2

--- a/solution.py
+++ b/solution.py
@@ -29,9 +29,9 @@
 
 
 def layer_kernel(act_hbm, routes_ref, weights_ref, gate_hbm, up_hbm, down_hbm, out_ref,
-                 xb, xr, gate_w, up_w, down_w, hid, part, recv, summed, back, final,
+                 xb, xr, gate_w, up_w, down_w, hid, part, recv, summed, back, home, landed,
                  w_sem, ws_sem, wr_sem, fs_sem, fr_sem, as_sem, ar_sem,
-                 rs_sem, rr_sem, bs_sem, br_sem, xs_sem, xr_sem, own_sem):
+                 rs_sem, rr_sem, bs_sem, br_sem, own_sem):
     section = lax.axis_index("section")
     place = lax.axis_index("expert")
     core = lax.rem(place, 2)
@@ -101,9 +101,10 @@
     def g_copy(way, dist, m, group):
         low, high = GROUPS[group]
         j = 0 if way == 1 else 1
-        hops = 2 if dist == 4 else 1
-        return pltpu.make_async_remote_copy(
-            src_ref=xb.at[SLOT[-(dist - hops) * way], m, :, low:high],
+        hops = 2 - dist % 2
+        source = 0 if dist <= 2 else 2
+        return pltpu.make_async_remote_copy(
+            src_ref=xb.at[SLOT[-source * way], m, :, low:high],
             dst_ref=xb.at[SLOT[-dist * way], m, :, low:high],
             send_sem=as_sem.at[j, dist - 1, m, group], recv_sem=ar_sem.at[j, dist - 1, m, group],
             device_id=g_peer(hops * way), device_id_type=MESH)
@@ -113,16 +114,17 @@
 
     def spread(group):
         for m in range(MICRO):
-            for way in WAYS:
-                start(g_copy(way, 1, m, group))
-
-    def relay(dist, group):
+            for dist in (2, 1):
+                for way in WAYS:
+                    start(g_copy(way, dist, m, group))
+
+    def relay(group):
         for m in range(MICRO):
             for way in WAYS:
-                g_copy(way, dist, m, group).wait_recv()
-                if dist == 2 and far(way, m):
+                g_copy(way, 2, m, group).wait_recv()
+                if far(way, m):
                     start(g_copy(way, 4, m, group))
-                start(g_copy(way, dist + 1, m, group))
+                start(g_copy(way, 3, m, group))
 
     def widen(slot, m):
         view = xb.at[slot, m].reshape(WIDE, UNIT, LANES)
@@ -163,38 +165,39 @@
         for m in range(MICRO):
             for i in range(*GROUPS[group]):
                 f_wait(m, ORDER[i])
-            for way in WAYS:
-                start(g_copy(way, 1, m, group))
+        spread(group)
 
     spread_from(1)
-    relay(1, 0)
+    relay(0)
     spread_from(2)
-    relay(1, 1)
     spread_from(3)
-    relay(2, 0)
-    relay(1, 2)
-    relay(2, 1)
-    relay(1, 3)
-    relay(2, 2)
-    relay(2, 3)
+    relay(1)
+    relay(2)
+    relay(3)
+    for m in range(MICRO):
+        for way in WAYS:
+            for group in range(4):
+                g_copy(way, 1, m, group).wait_recv()
+    def unit(slot, m):
+        row = m * HALF + slot * UNIT
+        return part.at[row:row + UNIT]
+
+    def back_copy(way, dist, m):
+        j = 0 if way == 1 else 1
+        return pltpu.make_async_remote_copy(
+            src_ref=unit(SLOT[dist * way], m), dst_ref=recv.at[j, dist - 1, m],
+            send_sem=rs_sem.at[j, dist - 1, m], recv_sem=rr_sem.at[j, dist - 1, m],
+            device_id=g_peer((2 - dist % 2) * way), device_id_type=MESH)
+
     for i in range(3):
         own_copies[i].wait()
-        w_out[i].wait()
+        w_out[i].wait_recv()
     for m in range(MICRO):
         for slot in range(5):
             widen(slot, m)
         compute(m, 0, 5)
-
-    def unit(slot, m):
-        row = m * HALF + slot * UNIT
-        return part.at[row:row + UNIT]
-
-    def back_copy(way, dist, m):
-        j = 0 if way == 1 else 1
-        return pltpu.make_async_remote_copy(
-            src_ref=unit(SLOT[dist * way], m), dst_ref=recv.at[j, dist - 1, m],
-            send_sem=rs_sem.at[j, dist - 1, m], recv_sem=rr_sem.at[j, dist - 1, m],
-            device_id=g_peer(2 * way if dist == 4 else way), device_id_type=MESH)
+        for way in WAYS:
+            start(back_copy(way, 1, m))
 
     for m in range(MICRO):
         for way in WAYS:
@@ -209,55 +212,61 @@
             if far(way, m):
                 start(back_copy(way, 4, m))
             start(back_copy(way, 3, m))
-    for dist in (2, 1):
-        for m in range(MICRO):
-            for way in WAYS:
-                j = 0 if way == 1 else 1
-                back_copy(way, dist + 1, m).wait_recv()
-                here = unit(SLOT[dist * way], m)
-                total = here[...].astype(F32) + recv[j, dist, m].astype(F32)
-                if dist == 2 and far(way, m):
-                    back_copy(way, 4, m).wait_recv()
-                    total = total + recv[j, 3, m].astype(F32)
-                here[...] = total.astype(BF16)
-                start(back_copy(way, dist, m))
+    for m in range(MICRO):
+        for way in WAYS:
+            j = 0 if way == 1 else 1
+            back_copy(way, 3, m).wait_recv()
+            here = unit(SLOT[2 * way], m)
+            total = here[...].astype(F32) + recv[j, 2, m].astype(F32)
+            if far(way, m):
+                back_copy(way, 4, m).wait_recv()
+                total = total + recv[j, 3, m].astype(F32)
+            here[...] = total.astype(BF16)
+            start(back_copy(way, 2, m))
+
+    def home_copy(m):
+        return pltpu.make_async_remote_copy(
+            src_ref=home.at[m], dst_ref=landed.at[m], send_sem=bs_sem.at[m, 0], recv_sem=br_sem.at[m, 0],
+            device_id=x_next, device_id_type=MESH)
 
     def f_back(m, k):
         return pltpu.make_async_remote_copy(
             src_ref=summed.at[m, :, SEAT[k]], dst_ref=back.at[m, :, SEAT[RING - k]],
             send_sem=bs_sem.at[m, k], recv_sem=br_sem.at[m, RING - k],
-            device_id=f_peer(k), device_id_type=MESH)
+            device_id=(x_next[0], f_peer(k)[1]), device_id_type=MESH)
 
     def f_back_wait(m, k):
         pltpu.make_async_remote_copy(
             src_ref=summed.at[m, :, SEAT[k]], dst_ref=back.at[m, :, SEAT[k]],
             send_sem=bs_sem.at[m, k], recv_sem=br_sem.at[m, k],
-            device_id=f_peer(k), device_id_type=MESH).wait_recv()
-
-    for m in range(MICRO):
-        back_copy(1, 1, m).wait_recv()
-        back_copy(-1, 1, m).wait_recv()
+            device_id=(x_next[0], f_peer(k)[1]), device_id_type=MESH).wait_recv()
+
+    for m in range(MICRO):
+        for way in WAYS:
+            for dist in (1, 2):
+                back_copy(way, dist, m).wait_recv()
         here = unit(0, m)
         for t in range(TILES):
             cols = slice(t * LANES, (t + 1) * LANES)
-            total = here[:, cols].astype(F32) + recv[0, 0, m, :, cols].astype(F32) + recv[1, 0, m, :, cols].astype(F32)
+            total = here[:, cols].astype(F32)
+            for dist in range(2):
+                total = total + recv[0, dist, m, :, cols].astype(F32) + recv[1, dist, m, :, cols].astype(F32)
+            home[m, t] = xb[0, m, t, 0].astype(F32) + total[0:ROWS]
             summed.at[m].reshape(TILES, UNIT, LANES)[t] = total.astype(BF16)
         for k in (4, 3, 5, 2, 6, 1, 7):
             start(f_back(m, k))
-    last = [pltpu.make_async_remote_copy(
-        src_ref=final.at[m], dst_ref=out_ref.at[m], send_sem=xs_sem.at[m], recv_sem=xr_sem.at[m],
-        device_id=x_next, device_id_type=MESH) for m in range(MICRO)]
-    for m in range(MICRO):
-        total = xb[0, m, 0:TILES, 0].astype(F32) + summed[m, :, 0].astype(F32)
+        start(home_copy(m))
+    for m in range(MICRO):
+        home_copy(m).wait_recv()
+        total = landed[m]
         for k in (1, 7, 2, 6, 3, 5, 4):
             f_back_wait(m, k)
             total = total + back[m, :, SEAT[k]].astype(F32)
-        final[m] = total.astype(BF16)
-        last[m].start()
+        out_ref[m] = total.astype(BF16)
     for copy in sent:
         copy.wait_send()
-    for m in range(MICRO):
-        last[m].wait()
+    for copy in w_out:
+        copy.wait_send()
 
 
 def on_device(activations, routes, gate_weights, w_gate, w_up, w_down):
@@ -281,13 +290,14 @@
             vmem((2, 4, MICRO, UNIT, D), BF16),
             vmem((MICRO, TILES, RING, ROWS, LANES), BF16),
             vmem((MICRO, TILES, RING, ROWS, LANES), BF16),
-            vmem((MICRO, TILES, ROWS, LANES), BF16),
+            vmem((MICRO, TILES, ROWS, LANES), F32),
+            vmem((MICRO, TILES, ROWS, LANES), F32),
             dma((3,)), dma((3,)), dma((3,)),
             dma((MICRO, RING)), dma((MICRO, RING)),
             dma((2, 4, MICRO, 4)), dma((2, 4, MICRO, 4)),
             dma((2, 4, MICRO)), dma((2, 4, MICRO)),
             dma((MICRO, RING)), dma((MICRO, RING)),
-            dma((MICRO,)), dma((MICRO,)), dma,
+            dma,
         ],
         compiler_params=pltpu.CompilerParams(
             collective_id=0, has_side_effects=True, vmem_limit_bytes=56 << 20),

time: 65.9 us -> 61.6 us (0.935)
  the two profiles are of different devices: /device:TPU:8 before, /device:TPU:16 now
where the time goes in v3:
time: 61.6 us; the launch traced here: 61.4 us
  Pallas kernels  60 us (97%)
  local copies, waits for them, and re-layouts  1.36 us (2%)
    pallas_call x1, Pallas kernels, on_device(): pl.pallas_call(layer_kernel, out_shape=jax.ShapeDtypeStruct((MICRO, TILES...  60 us
    unnamed x1, local copies, waits for them, and re-layouts  1.36 us

profile of v3, /device:TPU:16, one launch (start us, length us, event | category | flops | bytes accessed | tf_op | source)
XLA Modules:
  0.0 61.4 jit_solution(2987514343619655144)
XLA Ops:
  0.0 60.0 %shard_map.64 = bf16[2,24,2,128]{3,2,1,0:T(2,128)(2,1)} custom-call(bf16[2,24,2,128]{3,2,1,0:T(2,128)(2,1)} %bitcast.15, s32[2,2,2]{2,1,0:T(2,128)} %bitcast.16, f32[2,2,2]{2,1,0:T(2,128)} %bitcast.17, bf16[3072,256]{1,0:T(8,128)(2,1)} %bitcast.11, bf16[3072,256]{1,0:T(8,128)(2,1)} %bitcast.12, bf16[256,3072]{1,0:T(8,128)(2,1)} %bitcast.13), custom_call_target="tpu_custom_call" | custom-call | tf_op jit(solution)/shard_map/pallas_call | solution.py:276
  60.1 1.4 %copy.8 = bf16[1,2,2,3072]{3,2,1,0:T(2,128)(2,1)} copy(bf16[1,2,2,3072]{3,2,1,0:T(2,128)(2,1)} %bitcast.14) | data formatting | bytes 49152

commit v4 on v3

--- a/solution.py
+++ b/solution.py
@@ -25,6 +25,8 @@
 SEAT = {k: i for i, k in enumerate(ORDER)}
 GROUPS = ((0, 1), (1, 3), (3, 5), (5, 8))
 WAYS = (1, -1)
+LIGHT = ((1, 1), (0, -1))
+HEAVY = ((0, 1), (1, -1))
 HALF = RING * UNIT
 
 
@@ -101,8 +103,9 @@
     def g_copy(way, dist, m, group):
         low, high = GROUPS[group]
         j = 0 if way == 1 else 1
-        hops = 2 - dist % 2
-        source = 0 if dist <= 2 else 2
+        near = False
+        hops = 1 if near else 2 - dist % 2
+        source = 1 if near else 0 if dist <= 2 else 2
         return pltpu.make_async_remote_copy(
             src_ref=xb.at[SLOT[-source * way], m, :, low:high],
             dst_ref=xb.at[SLOT[-dist * way], m, :, low:high],
@@ -113,10 +116,16 @@
         return m == (0 if way == 1 else 1)
 
     def spread(group):
-        for m in range(MICRO):
-            for dist in (2, 1):
+        for dist in (2, 1):
+            for m in range(MICRO):
                 for way in WAYS:
                     start(g_copy(way, dist, m, group))
+
+    def pass_on(group):
+        for m in range(MICRO):
+            for way in WAYS:
+                g_copy(way, 1, m, group).wait_recv()
+                start(g_copy(way, 2, m, group))
 
     def relay(group):
         for m in range(MICRO):
@@ -128,15 +137,15 @@
 
     def widen(slot, m):
         view = xb.at[slot, m].reshape(WIDE, UNIT, LANES)
-        row = m * HALF + slot * UNIT
+        row = (slot * MICRO + m) * UNIT
         for t in range(WIDE):
             xr[row:row + UNIT, t * LANES:(t + 1) * LANES] = view[t]
 
     pick = lax.broadcasted_iota(jnp.int32, (LANES, HID), 0)
     pick = jnp.where((pick == expert) | (pick == expert + EXPERTS), 1.0, 0.0).astype(BF16)
 
-    def compute(m, low, high):
-        rows = slice(m * HALF + low * UNIT, m * HALF + high * UNIT)
+    def compute(low, high):
+        rows = slice(low * MICRO * UNIT, high * MICRO * UNIT)
         weight = jnp.dot(xr[rows, D:], pick, preferred_element_type=F32)
         for side in range(2):
             gate = jnp.dot(xr[rows, :D], gate_w[side], preferred_element_type=F32)
@@ -179,7 +188,7 @@
             for group in range(4):
                 g_copy(way, 1, m, group).wait_recv()
     def unit(slot, m):
-        row = m * HALF + slot * UNIT
+        row = (slot * MICRO + m) * UNIT
         return part.at[row:row + UNIT]
 
     def back_copy(way, dist, m):
@@ -195,7 +204,8 @@
     for m in range(MICRO):
         for slot in range(5):
             widen(slot, m)
-        compute(m, 0, 5)
+    compute(0, 5)
+    for m in range(MICRO):
         for way in WAYS:
             start(back_copy(way, 1, m))
 
@@ -207,22 +217,21 @@
                     g_copy(way, 4, m, group).wait_recv()
         for slot in range(5, 8):
             widen(slot, m)
-        compute(m, 5, 8)
-        for way in WAYS:
-            if far(way, m):
-                start(back_copy(way, 4, m))
-            start(back_copy(way, 3, m))
-    for m in range(MICRO):
-        for way in WAYS:
-            j = 0 if way == 1 else 1
-            back_copy(way, 3, m).wait_recv()
-            here = unit(SLOT[2 * way], m)
-            total = here[...].astype(F32) + recv[j, 2, m].astype(F32)
-            if far(way, m):
-                back_copy(way, 4, m).wait_recv()
-                total = total + recv[j, 3, m].astype(F32)
-            here[...] = total.astype(BF16)
-            start(back_copy(way, 2, m))
+    compute(5, 8)
+    for m, way in LIGHT + HEAVY:
+        if far(way, m):
+            start(back_copy(way, 4, m))
+        start(back_copy(way, 3, m))
+    for m, way in LIGHT + HEAVY:
+        j = 0 if way == 1 else 1
+        back_copy(way, 3, m).wait_recv()
+        here = unit(SLOT[2 * way], m)
+        total = here[...].astype(F32) + recv[j, 2, m].astype(F32)
+        if far(way, m):
+            back_copy(way, 4, m).wait_recv()
+            total = total + recv[j, 3, m].astype(F32)
+        here[...] = total.astype(BF16)
+        start(back_copy(way, 2, m))
 
     def home_copy(m):
         return pltpu.make_async_remote_copy(
@@ -231,13 +240,13 @@
 
     def f_back(m, k):
         return pltpu.make_async_remote_copy(
-            src_ref=summed.at[m, :, SEAT[k]], dst_ref=back.at[m, :, SEAT[RING - k]],
+            src_ref=summed.at[m, :, SEAT[k]], dst_ref=back.at[m, SEAT[RING - k]],
             send_sem=bs_sem.at[m, k], recv_sem=br_sem.at[m, RING - k],
             device_id=(x_next[0], f_peer(k)[1]), device_id_type=MESH)
 
     def f_back_wait(m, k):
         pltpu.make_async_remote_copy(
-            src_ref=summed.at[m, :, SEAT[k]], dst_ref=back.at[m, :, SEAT[k]],
+            src_ref=summed.at[m, :, SEAT[k]], dst_ref=back.at[m, SEAT[k]],
             send_sem=bs_sem.at[m, k], recv_sem=br_sem.at[m, k],
             device_id=(x_next[0], f_peer(k)[1]), device_id_type=MESH).wait_recv()
 
@@ -258,11 +267,11 @@
         start(home_copy(m))
     for m in range(MICRO):
         home_copy(m).wait_recv()
-        total = landed[m]
+        total = landed.at[m].reshape(TILES * ROWS, LANES)[...]
         for k in (1, 7, 2, 6, 3, 5, 4):
             f_back_wait(m, k)
-            total = total + back[m, :, SEAT[k]].astype(F32)
-        out_ref[m] = total.astype(BF16)
+            total = total + back.at[m, SEAT[k]].reshape(TILES * ROWS, LANES)[...].astype(F32)
+        out_ref[m * TILES * ROWS:(m + 1) * TILES * ROWS] = total
     for copy in sent:
         copy.wait_send()
     for copy in w_out:
@@ -275,7 +284,7 @@
     vmem = pltpu.VMEM
     out = pl.pallas_call(
         layer_kernel,
-        out_shape=jax.ShapeDtypeStruct((MICRO, TILES, ROWS, LANES), BF16),
+        out_shape=jax.ShapeDtypeStruct((MICRO * TILES * ROWS, LANES), F32),
         in_specs=[pl.BlockSpec(memory_space=pl.ANY)] + [pl.BlockSpec(memory_space=pltpu.VMEM)] * 2
         + [pl.BlockSpec(memory_space=pl.ANY)] * 3,
         out_specs=pl.BlockSpec(memory_space=pltpu.VMEM),
@@ -289,7 +298,7 @@
             vmem((MICRO * HALF, D), BF16),
             vmem((2, 4, MICRO, UNIT, D), BF16),
             vmem((MICRO, TILES, RING, ROWS, LANES), BF16),
-            vmem((MICRO, TILES, RING, ROWS, LANES), BF16),
+            vmem((MICRO, RING, TILES, ROWS, LANES), BF16),
             vmem((MICRO, TILES, ROWS, LANES), F32),
             vmem((MICRO, TILES, ROWS, LANES), F32),
             dma((3,)), dma((3,)), dma((3,)),
@@ -302,6 +311,7 @@
         compiler_params=pltpu.CompilerParams(
             collective_id=0, has_side_effects=True, vmem_limit_bytes=56 << 20),
     )(tokens, routes[0], gate_weights[0], w_gate[0], w_up[0], w_down[0])
+    out = out.astype(BF16).reshape(MICRO, TILES, ROWS, LANES)
     return out.transpose(0, 2, 1, 3).reshape(1, MICRO, ROWS, D)
 
 

time: 61.6 us -> 60.6 us (0.984)
  other arithmetic: 0 us -> 1.41 us
  local copies, waits for them, and re-layouts: 1.36 us -> 0 us
  Pallas kernels: 60 us -> 59 us
    convert_element_type x0 -> x1, other arithmetic: none -> 1.41 us  [on_device(): out = out.astype(BF16).reshape(MICRO, TILES, ROWS, LANES)]
    unnamed x1 -> x0, local copies, waits for them, and re-layouts: 1.36 us -> none
    pallas_call x1, Pallas kernels: 60 us -> 59 us  [on_device(): pl.pallas_call(layer_kernel, out_shape=jax.ShapeDtypeStruct((MICRO * TILE...]
where the time goes in v4:
time: 60.6 us; the launch traced here: 60.4 us
  Pallas kernels  59 us (97%)
  other arithmetic  1.41 us (2%)
    pallas_call x1, Pallas kernels, on_device(): pl.pallas_call(layer_kernel, out_shape=jax.ShapeDtypeStruct((MICRO * TILE...  59 us
    convert_element_type x1, other arithmetic, on_device(): out = out.astype(BF16).reshape(MICRO, TILES, ROWS, LANES)  1.41 us

profile of v4, /device:TPU:16, one launch (start us, length us, event | category | flops | bytes accessed | tf_op | source)
XLA Modules:
  0.0 60.4 jit_solution(11225963258162057306)
XLA Ops:
  0.0 59.0 %shard_map.64 = f32[96,128]{1,0:T(8,128)} custom-call(bf16[2,24,2,128]{3,2,1,0:T(2,128)(2,1)} %bitcast.16, s32[2,2,2]{2,1,0:T(2,128)} %bitcast.17, f32[2,2,2]{2,1,0:T(2,128)} %bitcast.18, bf16[3072,256]{1,0:T(8,128)(2,1)} %bitcast.13, bf16[3072,256]{1,0:T(8,128)(2,1)} %bitcast.14, bf16[256,3072]{1,0:T(8,128)(2,1)} %bitcast.15), custom_call_target="tpu_custom_call" | custom-call | tf_op jit(solution)/shard_map/pallas_call | solution.py:285
  59.0 1.4 %convert_element_type.3 = bf16[96,128]{1,0:T(8,128)(2,1)} convert(f32[96,128]{1,0:T(8,128)} %shard_map.64) | non-fusion elementwise | flops 12288 | bytes 73728 | tf_op jit(solution)/shard_map/convert_element_type | solution.py:314
